TPU v7x, 512 devices: a whole 4x8x8 slice. The times are simulated.
512 devices in a mesh: seq: 64 (over y, x, core), head: 8 (over z).
Axes of the slice: x: 4, y: 8, z: 8, core: 2. Of those that a mesh axis runs over, the one named last changes fastest.
Arguments:
- queries: bfloat16 [32768, 4096], P(('seq', 'head')), may hold values from -5 to 5
- new_keys: bfloat16 [32768, 1024], P(('seq', 'head')), may hold values from -12 to 12
- new_values: bfloat16 [32768, 1024], P(('seq', 'head')), may hold values from -6 to 6
- cache_keys: bfloat16 [131072, 1024], P('seq', 'head'), may hold values from -12 to 12
- cache_values: bfloat16 [131072, 1024], P('seq', 'head'), may hold values from -6 to 6
- tile_lists: int32 [256, 8, 12], P('seq', 'head'), may hold values from 0 to 1023, as said below
Outputs:
- attended: bfloat16 [32768, 4096], P(('seq', 'head'))
Inputs may be any that keep to these rules, and one draw needn't show every extreme that they name: `tile_lists`: for one key head, the 12 tiles of one block's list are distinct; the lists of the 4 blocks of one index of seq together name exactly 24 distinct tiles, at most 2 of them of one index of seq (tiles k * 16 to k * 16 + 15), and some index has exactly 2.
All inputs are finite; a program needn't handle non-finite values.
Results may differ from a plain program's by a relative error of at most 0.003.
Values may be sent and summed in bfloat16 or wider, within the bound.
A program may use at most 64 MiB of HBM per device.

v0:
```python
import math

import jax
import jax.numpy as jnp
from jax import lax
from jax.sharding import PartitionSpec as P

HQ = 32
KV = 8
HD = 128
QB = 128
TILE = 128
SEL = 12


NEG_FILL = -1e30


def passed_along(block, axis, distance):
    devices = range(lax.axis_size(axis))
    route = [(i - distance, i) for i in devices if i - distance in devices]
    return lax.ppermute(block, axis, route)


def pair_ranks(owners, tiles):
    pair_count = owners.shape[-1]
    earlier = jnp.arange(pair_count)[:, None] > jnp.arange(pair_count)[None, :]
    same_tile = tiles[..., :, None] == tiles[..., None, :]
    first_seen = jnp.logical_not(jnp.any(same_tile & earlier, axis=-1))
    same_owner = owners[..., :, None] == owners[..., None, :]
    smaller = tiles[..., None, :] < tiles[..., :, None]
    counted = same_owner & smaller & first_seen[..., None, :]
    return (jnp.sum(counted.astype(jnp.int32), axis=-1), first_seen)


def on_device(queries, new_keys, new_values, cache_keys, cache_values, tile_lists):
    q_rows, k_rows, v_rows = (
        lax.all_to_all(queries, "head", split_axis=1, concat_axis=0, tiled=True),
        lax.all_to_all(new_keys, "head", split_axis=1, concat_axis=0, tiled=True),
        lax.all_to_all(new_values, "head", split_axis=1, concat_axis=0, tiled=True),
    )
    rows_here = q_rows.shape[0]
    kv_here = k_rows.shape[1] // HD
    group_size = HQ // KV
    blocks_here = rows_here // QB
    tiles_here = cache_keys.shape[0] // TILE
    shards = lax.axis_size("seq")
    shard_index = lax.axis_index("seq")
    pair_total = blocks_here * SEL
    pool_size = max(SEL, pair_total // 2)
    capacity = max(2, (4 * pool_size + 3 * shards - 1) // (3 * shards))
    scale_factor = 1.0 / math.sqrt(HD)
    prior_keys, prior_values = passed_along(
        (k_rows[rows_here - QB :], v_rows[rows_here - QB :]), "seq", 1
    )
    pair_tiles = jnp.transpose(tile_lists, (1, 0, 2)).reshape(kv_here, pair_total)
    owners = pair_tiles // tiles_here
    pair_rank, first_seen = pair_ranks(owners, pair_tiles)
    every_list = lax.all_gather(tile_lists, "seq", axis=0, tiled=True)
    every_pair = jnp.transpose(
        every_list.reshape(shards, blocks_here, kv_here, SEL), (0, 2, 1, 3)
    ).reshape(shards, kv_here, pair_total)
    every_owner = every_pair // tiles_here
    every_rank, every_first = pair_ranks(every_owner, every_pair)
    own_hit = ((every_owner == shard_index) & every_first)[..., None]
    rank_hit = every_rank[..., None] == jnp.arange(capacity)
    marked = jnp.where(own_hit & rank_hit, (every_pair % tiles_here)[..., None] + 1, 0)
    asked_ids = jnp.sum(marked, axis=2) - 1
    head_pick = jnp.arange(kv_here)[None, :, None]
    filled = (asked_ids >= 0)[..., None, None]
    safe_ids = jnp.maximum(asked_ids, 0)
    key_tiles = jnp.transpose(cache_keys.reshape(tiles_here, TILE, kv_here, HD), (2, 0, 1, 3))
    value_tiles = jnp.transpose(cache_values.reshape(tiles_here, TILE, kv_here, HD), (2, 0, 1, 3))
    send_keys = jnp.where(filled, key_tiles[head_pick, safe_ids], jnp.zeros((), jnp.bfloat16))
    send_values = jnp.where(filled, value_tiles[head_pick, safe_ids], jnp.zeros((), jnp.bfloat16))
    causal = jnp.arange(QB)[:, None] >= jnp.arange(QB)[None, :]
    head_rows = jnp.arange(kv_here)[:, None]

    def local_part(block_index, source, prior_rows):
        current = lax.dynamic_slice_in_dim(source, block_index * QB, QB, 0)
        before_rows = lax.dynamic_slice_in_dim(source, jnp.maximum(block_index - 1, 0) * QB, QB, 0)
        previous = jnp.where(block_index == 0, prior_rows, before_rows)
        joined = jnp.concatenate([previous, current], axis=0).reshape(2 * QB, kv_here, HD)
        return jnp.transpose(joined, (1, 0, 2))

    def remote_part(block_index, received):
        block_owners = lax.dynamic_slice_in_dim(owners, block_index * SEL, SEL, 1)
        block_ranks = lax.dynamic_slice_in_dim(pair_rank, block_index * SEL, SEL, 1)
        return received[block_owners, head_rows, block_ranks].reshape(kv_here, SEL * TILE, HD)

    def block_weights(block_index, got_keys):
        query_block = lax.dynamic_slice_in_dim(q_rows, block_index * QB, QB, 0).reshape(
            QB, kv_here, group_size, HD
        )
        all_keys = jnp.concatenate(
            [remote_part(block_index, got_keys), local_part(block_index, k_rows, prior_keys)],
            axis=1,
        )
        scores = (
            jnp.einsum("qhgd,hkd->hgqk", query_block, all_keys, preferred_element_type=jnp.float32)
            * scale_factor
        )
        has_prior = jnp.broadcast_to((block_index > 0) | (shard_index > 0), (QB, QB))
        visible = jnp.concatenate(
            [jnp.ones((QB, SEL * TILE), dtype=bool), has_prior, causal], axis=1
        )
        masked = jnp.where(visible, scores, NEG_FILL)
        row_top = jnp.max(masked, axis=3, keepdims=True)
        exponent = jnp.exp(masked - row_top)
        row_total = jnp.sum(exponent, axis=3)
        return (exponent.astype(jnp.bfloat16), row_total)

    def block_output(block_index, weights, row_total, got_values):
        all_values = jnp.concatenate(
            [remote_part(block_index, got_values), local_part(block_index, v_rows, prior_values)],
            axis=1,
        )
        weighted = jnp.einsum(
            "hgqk,hkd->qhgd", weights, all_values, preferred_element_type=jnp.float32
        )
        result = weighted / jnp.transpose(row_total, (2, 0, 1))[..., None]
        return result.astype(jnp.bfloat16).reshape(QB, kv_here * group_size * HD)

    block_ids = jnp.arange(blocks_here)
    got_keys, got_values = (
        lax.all_to_all(send_keys, "seq", split_axis=0, concat_axis=0, tiled=True),
        lax.all_to_all(send_values, "seq", split_axis=0, concat_axis=0, tiled=True),
    )

    def whole_block(block_index):
        weights, row_total = block_weights(block_index, got_keys)
        return block_output(block_index, weights, row_total, got_values)

    outputs = lax.map(whole_block, block_ids)
    attended = outputs.reshape(rows_here, kv_here * group_size * HD)
    return lax.all_to_all(attended, "head", split_axis=0, concat_axis=1, tiled=True)


def solution(mesh):
    return jax.shard_map(
        on_device,
        mesh=mesh,
        in_specs=(
            P(("seq", "head"), None),
            P(("seq", "head"), None),
            P(("seq", "head"), None),
            P("seq", "head"),
            P("seq", "head"),
            P("seq", "head", None),
        ),
        out_specs=P(("seq", "head"), None),
        check_vma=False,
    )
```

profile of v0, /device:TPU:1, one launch (start us, length us, event | category | flops | bytes accessed | tf_op | source)
XLA Modules:
  0.0 395.9 jit_solution(17193188782176240120)
XLA Ops:
  0.0 1.6 copy_bitcast_fusion.2
  1.6 10.9 %all-to-all-start.1 = ((bf16[64,8,128]{2,0,1:T(8,128)(2,1)}), bf16[64,8,128]{2,0,1:T(8,128)(2,1)S(1)}, u32[]{:S(2)}, u32[]{:S(2)}) async-start(bf16[64,8,128]{2,0,1:T(8,128)(2,1)} %copy_bitcast_fusion.2), calls=%async_computation.1 | async-start | bytes 262144 | tf_op jit(solution)/shard_map/all_to_all | solution.py:40
  12.5 51.5 %all_gather.3 = s32[256,1,12]{2,1,0:T(1,128)S(1)} all-gather(s32[4,1,12]{2,1,0:T(1,128)} %param.13), channel_id=1, replica_groups=mesh['seq'=64,'head'=8] {'seq'}, dimensions={0}, use_global_device_ids=true | all-gather | bytes 12480 | tf_op jit(solution)/shard_map/all_gather | solution.py:59
  64.0 0.5 broadcast.762
  64.5 0.9 reduce.22
  65.6 0.5 and_reduce_fusion
  66.1 1.9 copy.90
  68.0 0.4 convert_reduce_fusion
  68.4 1.6 copy_bitcast_fusion.1
  70.0 6.9 %all-to-all-start.3 = ((bf16[64,8,128]{2,0,1:T(8,128)(2,1)}), bf16[64,8,128]{2,0,1:T(8,128)(2,1)S(1)}, u32[]{:S(2)}, u32[]{:S(2)}) async-start(bf16[64,8,128]{2,0,1:T(8,128)(2,1)} %copy_bitcast_fusion.1), calls=%async_computation.3 | async-start | bytes 262144 | tf_op jit(solution)/shard_map/all_to_all | solution.py:39
  76.9 8.3 %all-to-all-done.3 = bf16[64,8,128]{2,0,1:T(8,128)(2,1)S(1)} async-done(((bf16[64,8,128]{2,0,1:T(8,128)(2,1)}), bf16[64,8,128]{2,0,1:T(8,128)(2,1)S(1)}, u32[]{:S(2)}, u32[]{:S(2)}) %all-to-all-start.3) | async-done | bytes 131104 | tf_op jit(solution)/shard_map/all_to_all | solution.py:39
  85.3 3.5 all-to-all-start.4
  89.0 3.1 gather_fusion.2
  92.1 3.0 gather_fusion.3
  95.2 5.8 %broadcast_select_fusion = (bf16[64,1,2,128,128]{4,3,2,1,0:T(8,128)(2,1)}, bf16[64,1,2,128,128]{4,3,2,1,0:T(8,128)(2,1)}) fusion(bf16[64,1,2,128,128]{4,3,2,1,0:T(8,128)(2,1)} %bitcast.146, pred[64,2]{1,0:T(8,128)(4,1)S(1)} %copy.70, bf16[64,1,2,128,128]{4,3,2,1,0:T(8,128)(2,1)} %bitcast.145), kind=kLoop, calls=%fused_computation.42 | loop fusion | flops 4194304 | bytes 16777344 | tf_op jit(solution)/shard_map/jit(_where)/select_n | solution.py:74
  101.1 3.6 all-to-all-done.4
  104.7 104.1 %all_to_all.86 = bf16[64,1,2,128,128]{4,3,2,1,0:T(8,128)(2,1)} all-to-all(bf16[64,1,2,128,128]{4,3,2,1,0:T(8,128)(2,1)} %get-tuple-element.300), channel_id=1, replica_groups=mesh['seq'=64,'head'=8] {'seq'}, dimensions={0} | all-to-all | bytes 8388608 | tf_op jit(solution)/shard_map/all_to_all | solution.py:127
  208.8 7.3 %all-to-all-start.2 = ((bf16[64,1,2,128,128]{4,3,2,1,0:T(8,128)(2,1)}), bf16[64,1,2,128,128]{4,3,2,1,0:T(8,128)(2,1)}, u32[]{:S(2)}, u32[]{:S(2)}) async-start(bf16[64,1,2,128,128]{4,3,2,1,0:T(8,128)(2,1)} %get-tuple-element.299), calls=%async_computation.2 | async-start | bytes 8388608 | tf_op jit(solution)/shard_map/all_to_all | solution.py:126
  216.2 0.6 reduce.21
  216.9 0.2 fusion.28
  217.2 3.5 collective-permute-start
  220.7 2.1 collective-permute-start.1
  222.8 0.2 convert_reduce_fusion.1
  223.0 2.9 collective-permute-done
  225.9 0.8 collective-permute-done.1
  226.7 85.3 %all-to-all-done.2 = bf16[64,1,2,128,128]{4,3,2,1,0:T(8,128)(2,1)} async-done(((bf16[64,1,2,128,128]{4,3,2,1,0:T(8,128)(2,1)}), bf16[64,1,2,128,128]{4,3,2,1,0:T(8,128)(2,1)}, u32[]{:S(2)}, u32[]{:S(2)}) %all-to-all-start.2) | async-done | bytes 4194336 | tf_op jit(solution)/shard_map/all_to_all | solution.py:126
  312.0 65.0 %while.13 = (s32[]{:T(128)}, bf16[4,128,512]{2,1,0:T(8,128)(2,1)S(1)}, s32[4]{0:T(128)S(1)}, s32[1,48]{1,0:T(1,128)S(1)}, s32[1,48]{1,0:T(1,128)S(1)}, /*index=5...) while((s32[]{:T(128)}, ...), condition=%wide.region_8.9_spmd.clone, body=%wide.region_5.8_spmd.clone.sunk | while | flops 478692352 | bytes 31508588 | solution.py:134
  312.0 0.6 dynamic_slice.81
  315.1 2.9 gather_fusion
  318.8 0.3 pad_add_fusion.5
  319.1 0.6 fusion.47
  319.7 1.9 copy-done.1
  321.6 0.5 fusion.48
  322.2 2.9 gather_fusion.1
  325.1 0.2 copy.97
  325.3 2.8 fusion.49
  328.2 0.6 dynamic_slice.81
  331.4 2.9 gather_fusion
  335.0 0.3 pad_add_fusion.5
  335.3 0.6 fusion.47
  336.0 1.9 copy-done.1
  337.8 0.5 fusion.48
  338.5 2.9 gather_fusion.1
  341.3 0.2 copy.97
  341.5 2.8 fusion.49
  344.5 0.6 dynamic_slice.81
  347.6 2.9 gather_fusion
  351.3 0.3 pad_add_fusion.5
  351.6 0.6 fusion.47
  352.2 1.9 copy-done.1
  354.1 0.5 fusion.48
  354.7 2.9 gather_fusion.1
  357.8 2.8 fusion.49
  360.7 0.6 dynamic_slice.81
  363.9 2.9 gather_fusion
  367.5 0.3 pad_add_fusion.5
  367.8 0.6 fusion.47
  368.5 1.9 copy-done.1
  370.4 0.5 fusion.48
  371.0 2.9 gather_fusion.1
  373.8 0.2 copy.97
  374.0 2.8 fusion.49
  377.0 18.1 %all_to_all.87 = bf16[8,64,512]{2,1,0:T(8,128)(2,1)S(1)} all-to-all(bf16[8,64,512]{2,1,0:T(8,128)(2,1)S(1)} %bitcast.157), channel_id=1, replica_groups=mesh['seq'=64,'head'=8] {'head'}, dimensions={0} | all-to-all | bytes 1048576 | tf_op jit(solution)/shard_map/all_to_all | solution.py:136
  395.1 0.8 copy.86
  (98 shorter events, 3.8 us)
Async XLA Ops:
  0.0 89.0 %copy-start = (bf16[2048,128]{1,0:T(8,128)(2,1)S(1)}, bf16[2048,128]{1,0:T(8,128)(2,1)}, u32[]{:S(2)}) copy-start(bf16[2048,128]{1,0:T(8,128)(2,1)} %param.12) | copy-start | bytes 1572868
  1.6 68.4 %all-to-all-start.1 = ((bf16[64,8,128]{2,0,1:T(8,128)(2,1)}), bf16[64,8,128]{2,0,1:T(8,128)(2,1)S(1)}, u32[]{:S(2)}, u32[]{:S(2)}) async-start(bf16[64,8,128]{2,0,1:T(8,128)(2,1)} %copy_bitcast_fusion.2), calls=%async_computation.1 | async-start | bytes 262144 | tf_op jit(solution)/shard_map/all_to_all | solution.py:40
  70.0 15.3 %all-to-all-start.3 = ((bf16[64,8,128]{2,0,1:T(8,128)(2,1)}), bf16[64,8,128]{2,0,1:T(8,128)(2,1)S(1)}, u32[]{:S(2)}, u32[]{:S(2)}) async-start(bf16[64,8,128]{2,0,1:T(8,128)(2,1)} %copy_bitcast_fusion.1), calls=%async_computation.3 | async-start | bytes 262144 | tf_op jit(solution)/shard_map/all_to_all | solution.py:39
  85.3 19.4 %all-to-all-start.4 = ((bf16[64,8,512]{2,0,1:T(8,128)(2,1)}), bf16[64,8,512]{2,0,1:T(8,128)(2,1)S(1)}, u32[]{:S(2)}, u32[]{:S(2)}) async-start(bf16[64,8,512]{2,0,1:T(8,128)(2,1)} %bitcast.99), calls=%async_computation.4 | async-start | bytes 1048576 | tf_op jit(solution)/shard_map/all_to_all | solution.py:38
  89.0 3.1 copy-start.2
  208.8 7.4 %copy-start.3 = (s32[4,1,12]{2,1,0:T(1,128)S(1)}, s32[4,1,12]{2,1,0:T(1,128)}, u32[]{:S(2)}) copy-start(s32[4,1,12]{2,1,0:T(1,128)} %param.13) | copy-start | bytes 580
  208.8 103.1 %all-to-all-start.2 = ((bf16[64,1,2,128,128]{4,3,2,1,0:T(8,128)(2,1)}), bf16[64,1,2,128,128]{4,3,2,1,0:T(8,128)(2,1)}, u32[]{:S(2)}, u32[]{:S(2)}) async-start(bf16[64,1,2,128,128]{4,3,2,1,0:T(8,128)(2,1)} %get-tuple-element.299), calls=%async_computation.2 | async-start | bytes 8388608 | tf_op jit(solution)/shard_map/all_to_all | solution.py:126
  217.2 8.7 %collective-permute-start = (bf16[128,128]{1,0:T(8,128)(2,1)S(1)}, bf16[128,128]{1,0:T(8,128)(2,1)S(1)}, u32[]{:S(2)}, u32[]{:S(2)}) collective-permute-start(bf16[128,128]{1,0:T(8,128)(2,1)S(1)} %bitcast.159), channel_id=1, source_target_pairs={{0,8},{8,16},{16,24},{24,32},{32,40},{40,48},{48,56},{56,64},{64,7... | collective-permute-start | bytes 98312 | tf_op jit(solution)/shard_map/ppermute | solution.py:22
  220.7 5.9 %collective-permute-start.1 = (bf16[128,128]{1,0:T(8,128)(2,1)S(1)}, bf16[128,128]{1,0:T(8,128)(2,1)S(1)}, u32[]{:S(2)}, u32[]{:S(2)}) collective-permute-start(bf16[128,128]{1,0:T(8,128)(2,1)S(1)} %bitcast.160), channel_id=1, source_target_pairs={{0,8},{8,16},{16,24},{24,32},{32,40},{40,48},{48,56},{56,64},{64,7... | collective-permute-start | bytes 98312 | tf_op jit(solution)/shard_map/ppermute | solution.py:22
  319.7 1.9 copy-start.1
  336.0 1.9 copy-start.1
  352.2 1.9 copy-start.1
  368.5 1.9 copy-start.1
where the time goes:
time: 398 us; the launch traced here: 396 us
  blocking collectives  174 us (44%)
  waiting for transfers between devices  101 us (25%)
  local copies, waits for them, and re-layouts  48.2 us (12%)
  starting transfers between devices  34.2 us (9%)
  matrix products  13.7 us (3%)
  other arithmetic  12.8 us (3%)
  loops' own time  12.1 us (3%)
    all_to_all x1, blocking collectives, on_device(): lax.all_to_all(send_values, 'seq', split_axis=0, concat_axis=0, tiled=True)  104 us
    all_to_all x1, waiting for transfers between devices, on_device(): lax.all_to_all(send_keys, 'seq', split_axis=0, concat_axis=0, tiled=True)  85.3 us
    all_gather x1, blocking collectives, on_device(): every_list = lax.all_gather(tile_lists, 'seq', axis=0, tiled=True)  51.5 us
    gather x8, local copies, waits for them, and re-layouts, remote_part(): received[block_owners, head_rows, block_ranks]  22.8 us
    all_to_all x1, blocking collectives, on_device(): lax.all_to_all(attended, 'head', split_axis=0, concat_axis=1, tiled=True)  18.1 us
    another operation x1, loops' own time, on_device(): outputs = lax.map(whole_block, block_ids)  12.1 us
    dot_general x4, matrix products, block_output(): jnp.einsum('hgqk,hkd->qhgd', weights, all_values, preferred_element_type=...  11.2 us
    all_to_all x1, starting transfers between devices, on_device(): lax.all_to_all(new_values, 'head', split_axis=1, concat_axis=0, tiled=True)  10.9 us
  transfers between devices with their start and end apart: 6, of which 5 were waited for; matrix products, arithmetic and copies ran while one was open for 5% of the time, Pallas kernels for 0%

commit v1 on v0

v1 whole, which is shorter than its diff:
```python
import functools
import math

import jax
import jax.numpy as jnp
from jax import lax
from jax.experimental import pallas as pl
from jax.experimental.pallas import tpu as pltpu
from jax.sharding import PartitionSpec as P

KV = 8
HD = 128
QB = 128
TILE = 128
SEL = 12
GROUP = 4

RING = 8
ROW = 8
HEADS = 8
HELD = 16
CHUNK = 4
CHUNKS = HELD // CHUNK
BLOCKS = 4
ROWS = BLOCKS * QB
PART = ROWS // HEADS
WIDE = GROUP * HD
REMOTE = SEL * TILE
KEYS = REMOTE + 2 * QB
NEG_FILL = -1e30
EXP2_SCALE = math.log2(math.e) / math.sqrt(HD)
MESH = pl.DeviceIdType.MESH
ORDER = (2, 1, 3, 0)
SOFT_ROWS = 32


def kernel(
    q_in, k_in, v_in, key_tiles, value_tiles, list_in, slots,
    out,
    q_rows, k_loc, v_loc, row_lists, table, table_smem,
    kb1, kb2, kb3, kb4, kb5, kb6, kb7,
    vb1, vb2, vb3, vb4, vb5, vb6, vb7,
    stage, got_k, got_v, stacked, gathered, scores, weights, totals, out_stage,
    list_send, list_recv, plan_sem, y_send, y_recv, x_send, x_recv,
    z_send, z_recv, z_local, prev_send, prev_recv, o_send, o_recv, o_local,
):
    seq = lax.axis_index("seq")
    z = lax.axis_index("head")
    y = seq // ROW
    col = seq % ROW
    ahead = (seq + ROW) % (RING * ROW)
    behind = (seq + (RING - 1) * ROW) % (RING * ROW)
    after = (seq + 1) % (RING * ROW)
    before = (seq + RING * ROW - 1) % (RING * ROW)
    blocks_of = ((key_tiles, kb1, kb2, kb3, kb4, kb5, kb6, kb7), (value_tiles, vb1, vb2, vb3, vb4, vb5, vb6, vb7))
    got = (got_k, got_v)

    def row_peer(o):
        return y * ROW + (col + o) % ROW

    def head_peer(o):
        return (z + o) % HEADS

    barrier = pltpu.get_barrier_semaphore()

    def greet(where):
        pl.semaphore_signal(barrier, inc=1, device_id=where, device_id_type=MESH)

    for o in range(1, ROW):
        greet((row_peer(o), z))
    for o in range(1, HEADS):
        greet((seq, head_peer(o)))
    greet((ahead, z))
    greet((behind, z))
    greet((before, HEADS - 2))
    greet((before, HEADS - 1))
    is_last = z >= HEADS - 2
    pl.semaphore_wait(barrier, ROW - 1 + HEADS - 1 + 2 + jnp.where(is_last, HEADS, 0))

    def remote(src, dst, send, recv, where):
        return pltpu.make_async_remote_copy(
            src_ref=src, dst_ref=dst, send_sem=send, recv_sem=recv, device_id=where, device_id_type=MESH
        )

    def list_copy(o):
        return remote(list_in, row_lists.at[col], list_send.at[o - 1], list_recv.at[o - 1], (row_peer(o), z))

    def ring_copy(kv, way, hop, chunk):
        refs = blocks_of[kv]
        if way == 0:
            src, dst, where = refs[hop - 1], refs[hop], ahead
        else:
            src, dst, where = refs[(RING - hop + 1) % RING], refs[RING - hop], behind
        part = pl.ds(chunk * CHUNK, CHUNK)
        return remote(
            src.at[part], dst.at[part], y_send.at[kv, way, hop - 1, chunk], y_recv.at[kv, way, hop - 1, chunk], (where, z)
        )

    def row_copy(kv, rel, o):
        return remote(
            stage.at[kv, rel, o - 1],
            got[kv].at[pl.ds(col * 2 * RING + 2 * rel, 2)],
            x_send.at[kv, rel, o - 1],
            x_recv.at[kv, rel, o - 1],
            (row_peer(o), z),
        )

    def head_copies(o):
        to = head_peer(o)
        wide = pl.ds(pl.multiple_of(to * WIDE, WIDE), WIDE)
        narrow = pl.ds(pl.multiple_of(to * HD, HD), HD)
        rows = pl.ds(pl.multiple_of(z * PART, PART), PART)
        new_rows = pl.ds(pl.multiple_of(QB + z * PART, PART), PART)
        triples = ((q_in.at[:, wide], q_rows.at[rows]), (k_in.at[:, narrow], k_loc.at[new_rows]), (v_in.at[:, narrow], v_loc.at[new_rows]))
        if o == 0:
            return [pltpu.make_async_copy(src, dst, z_local.at[i]) for i, (src, dst) in enumerate(triples)]
        return [
            remote(src, dst, z_send.at[i, o - 1], z_recv.at[i, o - 1], (seq, to)) for i, (src, dst) in enumerate(triples)
        ]

    def prior_copies(to):
        source = z % 2
        narrow = pl.ds(to * HD, HD)
        rows = pl.ds(pl.multiple_of(source * PART, PART), PART)
        return [
            remote(k_in.at[:, narrow], k_loc.at[rows], prev_send.at[0, to], prev_recv.at[0, source], (after, to)),
            remote(v_in.at[:, narrow], v_loc.at[rows], prev_send.at[1, to], prev_recv.at[1, source], (after, to)),
        ]

    def forward(kv, hop, chunks):
        for chunk in chunks:
            ring_copy(kv, 0, hop, chunk).start()
            ring_copy(kv, 1, hop, chunk).start()

    for o in range(1, ROW):
        list_copy(o).start()
    forward(0, 1, range(CHUNKS))
    for o in range(HEADS):
        for copy in head_copies(o):
            copy.start()

    @pl.when(is_last)
    def _():
        for to in range(HEADS):
            for copy in prior_copies(to):
                copy.start()

    for o in range(1, ROW):
        list_copy(o).wait()
    row_lists[col] = list_in[...]
    lane = lax.broadcasted_iota(jnp.int32, (ROW, 128), 1)
    device = lax.broadcasted_iota(jnp.int32, (ROW, 128), 0)
    listed = row_lists[0]
    for d in range(1, ROW):
        listed = jnp.where(device == d, row_lists[d], listed)
    plan = jnp.zeros((ROW, 128), jnp.int32)
    for rel in range(RING):
        owner = ((y + RING - rel) % RING) * ROW + col
        mine = lax.shift_right_arithmetic(listed, 4) == owner
        tile = jnp.bitwise_and(listed, HELD - 1)
        smallest = jnp.min(jnp.where(mine, tile, HELD - 1), axis=1, keepdims=True)
        largest = jnp.max(jnp.where(mine, tile, 0), axis=1, keepdims=True)
        plan = jnp.where(lane == 2 * rel, smallest, plan)
        plan = jnp.where(lane == 2 * rel + 1, largest, plan)
    table[...] = plan

    def pack(kv, rel):
        source = blocks_of[kv][rel]

        def one(o, carry):
            to = (col + o) % ROW
            for rank in range(2):
                pick = jnp.bitwise_and(table_smem[to, 2 * rel + rank], HELD - 1)
                stage[kv, rel, o - 1, rank] = source[pick]
            return carry

        lax.fori_loop(1, ROW, one, 0)
        for rank in range(2):
            pick = jnp.bitwise_and(table_smem[col, 2 * rel + rank], HELD - 1)
            got[kv][col * 2 * RING + 2 * rel + rank] = source[pick]

    def hand_out(kv, rel):
        for o in range(1, ROW):
            row_copy(kv, rel, o).start()

    def travel(kv, first):
        packed = []
        for hop in range(1, 4):
            for chunk in range(CHUNKS):
                for way in range(2):
                    ring_copy(kv, way, hop, chunk).wait_recv()
                    if hop < 3 or (chunk < CHUNKS // 2) == (way == 0):
                        ring_copy(kv, way, hop + 1, chunk).start()
                if hop == 1 and chunk == 0:
                    first()
                    pack(kv, 0)
                    packed.append(0)
                if chunk == 1:
                    for rel in packed:
                        hand_out(kv, rel)
                    packed = []
            pack(kv, hop)
            pack(kv, RING - hop)
            packed += [hop, RING - hop]
        return packed

    def arrive(kv):
        for chunk in range(CHUNKS // 2):
            ring_copy(kv, 0, 4, chunk).wait_recv()
            ring_copy(kv, 1, 4, CHUNKS // 2 + chunk).wait_recv()
        pack(kv, 4)

    def read_plan():
        copy = pltpu.make_async_copy(table, table_smem, plan_sem)
        copy.start()
        copy.wait()

    packed = travel(0, read_plan)
    forward(1, 1, range(CHUNKS))
    for rel in packed:
        hand_out(0, rel)
    arrive(0)
    hand_out(0, 4)

    packed = travel(1, lambda: None)
    for rel in packed:
        hand_out(1, rel)
    arrive(1)
    hand_out(1, 4)

    for copy in head_copies(0):
        copy.wait()
    for o in range(1, HEADS):
        for copy in head_copies(o):
            copy.wait()
    for source in range(2):
        rows = pl.ds(source * PART, PART)
        for kv, ref in enumerate((k_loc, v_loc)):
            pltpu.make_async_copy(ref.at[rows], ref.at[rows], prev_recv.at[kv, source]).wait()
    for rel in range(RING):
        for o in range(1, ROW):
            row_copy(0, rel, o).wait()

    def block_at(step):
        return (z // 2 + step) % BLOCKS

    def gather(source, block):
        def one(j, carry):
            pick = jnp.bitwise_and(slots[block * SEL + j], 2 * RING * ROW - 1)
            gathered[pl.ds(pl.multiple_of(j * TILE, TILE), TILE), :] = source[pick]
            return carry

        lax.fori_loop(0, SEL, one, 0)

    def score(step, carry):
        block = block_at(step)
        first_row = pl.multiple_of(block * QB, QB)
        gather(got_k, block)
        for h in range(GROUP):
            stacked[pl.ds(h * QB, QB), :] = q_rows[pl.ds(first_row, QB), pl.ds(h * HD, HD)]
        contract = (((1,), (1,)), ((), ()))
        gathered[pl.ds(REMOTE, 2 * QB), :] = k_loc[pl.ds(first_row, 2 * QB), :]
        for pair in range(KEYS // (2 * TILE)):
            part = pl.ds(pair * 2 * TILE, 2 * TILE)
            scores[:, part] = lax.dot_general(stacked[...], gathered[part, :], contract, preferred_element_type=jnp.float32)
        from_column = jnp.where(block + seq > 0, 0, QB)
        row = lax.broadcasted_iota(jnp.int32, (SOFT_ROWS, 2 * QB), 0)
        column = lax.broadcasted_iota(jnp.int32, (SOFT_ROWS, 2 * QB), 1)

        def soften(i, inner):
            first = pl.multiple_of(i * SOFT_ROWS, SOFT_ROWS)
            rows = pl.ds(first, SOFT_ROWS)
            visible = (column - QB <= row + first % QB) & (column >= from_column)
            far = scores[rows, pl.ds(0, REMOTE)]
            near = jnp.where(visible, scores[rows, pl.ds(REMOTE, 2 * QB)], NEG_FILL)
            top = jnp.maximum(jnp.max(far, axis=1, keepdims=True), jnp.max(near, axis=1, keepdims=True))
            far = jnp.exp2((far - top) * EXP2_SCALE)
            near = jnp.exp2((near - top) * EXP2_SCALE)
            total = jnp.sum(far, axis=1, keepdims=True) + jnp.sum(near, axis=1, keepdims=True)
            weights[step, rows, pl.ds(0, REMOTE)] = far.astype(jnp.bfloat16)
            weights[step, rows, pl.ds(REMOTE, 2 * QB)] = near.astype(jnp.bfloat16)
            totals[step, rows, :] = jnp.broadcast_to(total, (SOFT_ROWS, HD))
            return inner

        return lax.fori_loop(0, GROUP * QB // SOFT_ROWS, soften, carry)

    lax.fori_loop(0, BLOCKS, score, 0)

    for rel in range(RING):
        for o in range(1, ROW):
            row_copy(1, rel, o).wait()

    def out_copy(to, place):
        rows = pl.ds(pl.multiple_of(to * PART, PART), PART)
        wide = pl.ds(pl.multiple_of(z * WIDE, WIDE), WIDE)
        return out_stage.at[rows], out.at[:, wide], place, to

    def attend(step):
        block = block_at(step)
        first_row = pl.multiple_of(block * QB, QB)
        gather(got_v, block)
        gathered[pl.ds(REMOTE, 2 * QB), :] = v_loc[pl.ds(first_row, 2 * QB), :]
        total = jnp.dot(weights[step], gathered[...], preferred_element_type=jnp.float32)
        result = (total / totals[step]).astype(jnp.bfloat16)
        for h in range(GROUP):
            out_stage[pl.ds(first_row, QB), pl.ds(h * HD, HD)] = result[h * QB : (h + 1) * QB]

    returns = []
    for step in ORDER:
        attend(step)
        if step != 0:
            for half in range(2):
                to = 2 * block_at(step) + half
                place = 2 * step + (z + half) % 2
                copy = out_copy(to, place)
                returns.append(remote(copy[0], copy[1], o_send.at[place], o_recv.at[place], (seq, to)))
                returns[-1].start()
        else:
            to = z + 1 - 2 * (z % 2)
            copy = out_copy(to, 0)
            returns.append(remote(copy[0], copy[1], o_send.at[0], o_recv.at[0], (seq, to)))
            returns[-1].start()
            own = out_copy(z, 0)
            local = pltpu.make_async_copy(own[0], own[1], o_local)
            local.start()
    local.wait()
    for copy in returns:
        copy.wait()

    for kv in range(2):
        for hop in range(1, 5):
            for chunk in range(CHUNKS):
                for way in range(2):
                    if hop < 4 or (chunk < CHUNKS // 2) == (way == 0):
                        ring_copy(kv, way, hop, chunk).wait_send()

    @pl.when(is_last)
    def _():
        for to in range(HEADS):
            for copy in prior_copies(to):
                copy.wait_send()


def on_device(queries, new_keys, new_values, cache_keys, cache_values, tile_lists):
    y = lax.axis_index("seq") // ROW
    listed = tile_lists.reshape(BLOCKS * SEL)
    list_in = jnp.broadcast_to(
        jnp.pad(listed, (0, 128 - BLOCKS * SEL), constant_values=-1)[None, :], (8, 128)
    )
    owner = listed // HELD
    not_smallest = jnp.any((owner[:, None] == owner[None, :]) & (listed[None, :] < listed[:, None]), axis=1)
    rel = (y - owner // ROW) % RING
    slots = ((owner % ROW) * RING + rel) * 2 + not_smallest.astype(jnp.int32)

    tiles = pltpu.VMEM((HELD, TILE, HD), jnp.bfloat16)
    dma = pltpu.SemaphoreType.DMA
    vmem = pl.BlockSpec(memory_space=pltpu.VMEM)
    return pl.pallas_call(
        kernel,
        out_shape=jax.ShapeDtypeStruct((PART, HEADS * WIDE), jnp.bfloat16),
        in_specs=[vmem] * 6 + [pl.BlockSpec(memory_space=pltpu.SMEM)],
        out_specs=vmem,
        scratch_shapes=[
            pltpu.VMEM((ROWS, WIDE), jnp.bfloat16),
            pltpu.VMEM((QB + ROWS, HD), jnp.bfloat16),
            pltpu.VMEM((QB + ROWS, HD), jnp.bfloat16),
            pltpu.VMEM((ROW, 8, 128), jnp.int32),
            pltpu.VMEM((ROW, 128), jnp.int32),
            pltpu.SMEM((ROW, 128), jnp.int32),
            *([tiles] * 14),
            pltpu.VMEM((2, RING, ROW - 1, 2, TILE, HD), jnp.bfloat16),
            pltpu.VMEM((2 * RING * ROW, TILE, HD), jnp.bfloat16),
            pltpu.VMEM((2 * RING * ROW, TILE, HD), jnp.bfloat16),
            pltpu.VMEM((GROUP * QB, HD), jnp.bfloat16),
            pltpu.VMEM((KEYS, HD), jnp.bfloat16),
            pltpu.VMEM((GROUP * QB, KEYS), jnp.float32),
            pltpu.VMEM((BLOCKS, GROUP * QB, KEYS), jnp.bfloat16),
            pltpu.VMEM((BLOCKS, GROUP * QB, HD), jnp.float32),
            pltpu.VMEM((ROWS, WIDE), jnp.bfloat16),
            dma((ROW - 1,)),
            dma((ROW - 1,)),
            dma,
            dma((2, 2, 4, CHUNKS)),
            dma((2, 2, 4, CHUNKS)),
            dma((2, RING, ROW - 1)),
            dma((2, RING, ROW - 1)),
            dma((3, HEADS - 1)),
            dma((3, HEADS - 1)),
            dma((3,)),
            dma((2, HEADS)),
            dma((2, 2)),
            dma((HEADS,)),
            dma((HEADS,)),
            dma,
        ],
        compiler_params=pltpu.CompilerParams(
            collective_id=0, has_side_effects=True, vmem_limit_bytes=64000 * 1024
        ),
    )(
        queries,
        new_keys,
        new_values,
        cache_keys.reshape(HELD, TILE, HD),
        cache_values.reshape(HELD, TILE, HD),
        list_in,
        slots,
    )


def solution(mesh):
    return jax.shard_map(
        on_device,
        mesh=mesh,
        in_specs=(
            P(("seq", "head"), None),
            P(("seq", "head"), None),
            P(("seq", "head"), None),
            P("seq", "head"),
            P("seq", "head"),
            P("seq", "head", None),
        ),
        out_specs=P(("seq", "head"), None),
        check_vma=False,
    )
```

time: 398 us -> 146 us (0.37)
  blocking collectives: 174 us -> 0 us
  Pallas kernels: 0 us -> 141 us
  waiting for transfers between devices: 101 us -> 0 us
  local copies, waits for them, and re-layouts: 48.2 us -> 3.24 us
  starting transfers between devices: 34.2 us -> 0 us
  matrix products: 13.7 us -> 0 us
  loops' own time: 12.1 us -> 0 us
  other arithmetic: 12.8 us -> 1.49 us
    pallas_call x0 -> x1, Pallas kernels: none -> 141 us  [on_device(): pl.pallas_call(kernel, out_shape=jax.ShapeDtypeStruct((PART, HEADS * WIDE...]
    all_to_all x2 -> x0, blocking collectives: 122 us -> none  [the longest x1 104 us: on_device(): lax.all_to_all(send_values, 'seq', split_axis=0, concat_axis=0, tiled=True)]
    all_to_all x4 -> x0, waiting for transfers between devices: 97.2 us -> none  [the longest x1 85.3 us: on_device(): lax.all_to_all(send_keys, 'seq', split_axis=0, concat_axis=0, tiled=True)]
    all_gather x1 -> x0, blocking collectives: 51.5 us -> none  [on_device(): every_list = lax.all_gather(tile_lists, 'seq', axis=0, tiled=True)]
    gather x10 -> x0, local copies, waits for them, and re-layouts: 28.9 us -> none  [the longest x8 22.8 us: remote_part(): received[block_owners, head_rows, block_ranks]]
    all_to_all x4 -> x0, starting transfers between devices: 28.6 us -> none  [the longest x1 10.9 us: on_device(): lax.all_to_all(new_values, 'head', split_axis=1, concat_axis=0, tiled=True)]
    dot_general x8 -> x0, matrix products: 13.7 us -> none  [the longest x4 11.2 us: block_output(): jnp.einsum('hgqk,hkd->qhgd', weights, all_values, preferred_element_type=...]
    another operation x1 -> x0, loops' own time: 12.1 us -> none  [on_device(): outputs = lax.map(whole_block, block_ids)]
  transfers between devices with their start and end apart: 6 -> 0, of which waited for: 5 -> 0; matrix products, arithmetic and copies ran while one was open for 5% -> 0% of each run, Pallas kernels for 0% -> 0%
where the time goes in v1:
time: 146 us; the launch traced here: 145 us
  Pallas kernels  141 us (97%)
  local copies, waits for them, and re-layouts  3.24 us (2%)
  other arithmetic  1.49 us (1%)
    pallas_call x1, Pallas kernels, on_device(): pl.pallas_call(kernel, out_shape=jax.ShapeDtypeStruct((PART, HEADS * WIDE...  141 us

profile of v1, /device:TPU:1, one launch (start us, length us, event | category | flops | bytes accessed | tf_op | source)
XLA Modules:
  0.0 145.4 jit_solution(12888174760325483854)
XLA Ops:
  0.0 0.0 copy-start
  0.0 0.5 broadcast.79
  0.5 0.2 copy-done
  0.7 0.7 reduce.3
  1.3 0.1 reshape.70
  1.4 0.2 and_reduce_fusion
  1.6 0.6 convert_add_fusion.slots
  2.3 0.6 broadcast_in_dim.2.list_in
  2.9 140.7 %shard_map.64 = bf16[64,4096]{1,0:T(8,128)(2,1)} custom-call(bf16[64,4096]{1,0:T(8,128)(2,1)} %q_in.1, bf16[64,1024]{1,0:T(8,128)(2,1)} %k_in.1, bf16[64,1024]{1,0:T(8,128)(2,1)} %v_in.1, bf16[16,128,128]{2,1,0:T(8,128)(2,1)} %bitcast.2, bf16[16,128,128]{2,1,0:T(8,128)(2,1)} %bitcast.3, s32[8,128]{1,0:T(8,128)} %broadcast_in_dim.2.list_in, ...), custom_call_target="tpu_custom_call" | custom-call | tf_op jit(solution)/shard_map/pallas_call | solution.py:358
  143.5 1.9 %copy.8 = bf16[64,4096]{1,0:T(8,128)(2,1)} copy(bf16[64,4096]{1,0:T(8,128)(2,1)} %shard_map.64) | data formatting | bytes 1048576
  (2 shorter events, 0.0 us)
Async XLA Ops:
  0.0 0.7 copy-start

commit v2 on v1

--- a/solution.py
+++ b/solution.py
@@ -35,13 +35,13 @@
 
 
 def kernel(
-    q_in, k_in, v_in, key_tiles, value_tiles, list_in, slots,
+    q_in, k_in, v_in, key_tiles, value_tiles, lists,
     out,
-    q_rows, k_loc, v_loc, row_lists, table, table_smem,
+    q_rows, k_loc, v_loc, list_raw, list_in, row_lists, table, table_smem, slot_table, slots,
     kb1, kb2, kb3, kb4, kb5, kb6, kb7,
     vb1, vb2, vb3, vb4, vb5, vb6, vb7,
     stage, got_k, got_v, stacked, gathered, scores, weights, totals, out_stage,
-    list_send, list_recv, plan_sem, y_send, y_recv, x_send, x_recv,
+    list_send, list_recv, plan_sem, slot_sem, y_send, y_recv, x_send, x_recv,
     z_send, z_recv, z_local, prev_send, prev_recv, o_send, o_recv, o_local,
 ):
     seq = lax.axis_index("seq")
@@ -61,6 +61,18 @@
     def head_peer(o):
         return (z + o) % HEADS
 
+    lane = lax.broadcasted_iota(jnp.int32, (ROW, 128), 1)
+    device = lax.broadcasted_iota(jnp.int32, (ROW, 128), 0)
+    list_raw[...] = jnp.full((8, 128), -1, jnp.int32)
+    for block in range(BLOCKS):
+        list_raw[pl.ds(block, 1), pl.ds(0, SEL)] = lists[block]
+    raw = list_raw[...]
+    flat = jnp.full((8, 128), -1, jnp.int32)
+    for block in range(BLOCKS):
+        moved = pltpu.roll(jnp.broadcast_to(raw[block : block + 1], (8, 128)), block * SEL, 1)
+        flat = jnp.where((lane >= block * SEL) & (lane < (block + 1) * SEL), moved, flat)
+    list_in[...] = flat
+
     barrier = pltpu.get_barrier_semaphore()
 
     def greet(where):
@@ -148,8 +160,6 @@
     for o in range(1, ROW):
         list_copy(o).wait()
     row_lists[col] = list_in[...]
-    lane = lax.broadcasted_iota(jnp.int32, (ROW, 128), 1)
-    device = lax.broadcasted_iota(jnp.int32, (ROW, 128), 0)
     listed = row_lists[0]
     for d in range(1, ROW):
         listed = jnp.where(device == d, row_lists[d], listed)
@@ -164,6 +174,18 @@
         plan = jnp.where(lane == 2 * rel + 1, largest, plan)
     table[...] = plan
 
+    entries = BLOCKS * SEL
+    across = jnp.broadcast_to(flat[0:1], (entries, 128))
+    lanes = lax.broadcasted_iota(jnp.int32, (entries, 128), 1)
+    diagonal = lanes == lax.broadcasted_iota(jnp.int32, (entries, 128), 0)
+    down = jnp.max(jnp.where(diagonal, across, 0), axis=1, keepdims=True)
+    owner = lax.shift_right_arithmetic(down, 4)
+    earlier = (lax.shift_right_arithmetic(across, 4) == owner) & (across < down)
+    rank = jnp.max(jnp.where(earlier, 1, 0), axis=1, keepdims=True)
+    rel = jnp.bitwise_and(y - lax.shift_right_arithmetic(owner, 3), RING - 1)
+    slot = (jnp.bitwise_and(owner, ROW - 1) * RING + rel) * 2 + rank
+    slot_table[...] = jnp.broadcast_to(slot, (entries, 128))
+
     def pack(kv, rel):
         source = blocks_of[kv][rel]
 
@@ -183,8 +205,7 @@
         for o in range(1, ROW):
             row_copy(kv, rel, o).start()
 
-    def travel(kv, first):
-        packed = []
+    def travel(kv, first, packed):
         for hop in range(1, 4):
             for chunk in range(CHUNKS):
                 for way in range(2):
@@ -193,15 +214,14 @@
                         ring_copy(kv, way, hop + 1, chunk).start()
                 if hop == 1 and chunk == 0:
                     first()
-                    pack(kv, 0)
-                    packed.append(0)
-                if chunk == 1:
-                    for rel in packed:
-                        hand_out(kv, rel)
+                if chunk == (1 if hop == 1 else 0):
+                    for ready in packed:
+                        hand_out(*ready)
                     packed = []
             pack(kv, hop)
             pack(kv, RING - hop)
-            packed += [hop, RING - hop]
+            hand_out(kv, hop)
+            packed.append((kv, RING - hop))
         return packed
 
     def arrive(kv):
@@ -214,17 +234,23 @@
         copy = pltpu.make_async_copy(table, table_smem, plan_sem)
         copy.start()
         copy.wait()
-
-    packed = travel(0, read_plan)
+        for kv in range(2):
+            pack(kv, 0)
+        hand_out(0, 0)
+
+    packed = travel(0, read_plan, [(1, 0)])
+    copy = pltpu.make_async_copy(slot_table, slots, slot_sem)
+    copy.start()
+    copy.wait()
     forward(1, 1, range(CHUNKS))
-    for rel in packed:
-        hand_out(0, rel)
+    for ready in packed:
+        hand_out(*ready)
     arrive(0)
     hand_out(0, 4)
 
-    packed = travel(1, lambda: None)
-    for rel in packed:
-        hand_out(1, rel)
+    packed = travel(1, lambda: None, [])
+    for ready in packed:
+        hand_out(*ready)
     arrive(1)
     hand_out(1, 4)
 
@@ -246,7 +272,7 @@
 
     def gather(source, block):
         def one(j, carry):
-            pick = jnp.bitwise_and(slots[block * SEL + j], 2 * RING * ROW - 1)
+            pick = jnp.bitwise_and(slots[block * SEL + j, 0], 2 * RING * ROW - 1)
             gathered[pl.ds(pl.multiple_of(j * TILE, TILE), TILE), :] = source[pick]
             return carry
 
@@ -342,31 +368,25 @@
 
 
 def on_device(queries, new_keys, new_values, cache_keys, cache_values, tile_lists):
-    y = lax.axis_index("seq") // ROW
-    listed = tile_lists.reshape(BLOCKS * SEL)
-    list_in = jnp.broadcast_to(
-        jnp.pad(listed, (0, 128 - BLOCKS * SEL), constant_values=-1)[None, :], (8, 128)
-    )
-    owner = listed // HELD
-    not_smallest = jnp.any((owner[:, None] == owner[None, :]) & (listed[None, :] < listed[:, None]), axis=1)
-    rel = (y - owner // ROW) % RING
-    slots = ((owner % ROW) * RING + rel) * 2 + not_smallest.astype(jnp.int32)
-
     tiles = pltpu.VMEM((HELD, TILE, HD), jnp.bfloat16)
     dma = pltpu.SemaphoreType.DMA
     vmem = pl.BlockSpec(memory_space=pltpu.VMEM)
     return pl.pallas_call(
         kernel,
         out_shape=jax.ShapeDtypeStruct((PART, HEADS * WIDE), jnp.bfloat16),
-        in_specs=[vmem] * 6 + [pl.BlockSpec(memory_space=pltpu.SMEM)],
+        in_specs=[vmem] * 6,
         out_specs=vmem,
         scratch_shapes=[
             pltpu.VMEM((ROWS, WIDE), jnp.bfloat16),
             pltpu.VMEM((QB + ROWS, HD), jnp.bfloat16),
             pltpu.VMEM((QB + ROWS, HD), jnp.bfloat16),
+            pltpu.VMEM((8, 128), jnp.int32),
+            pltpu.VMEM((8, 128), jnp.int32),
             pltpu.VMEM((ROW, 8, 128), jnp.int32),
             pltpu.VMEM((ROW, 128), jnp.int32),
             pltpu.SMEM((ROW, 128), jnp.int32),
+            pltpu.VMEM((BLOCKS * SEL, 128), jnp.int32),
+            pltpu.SMEM((BLOCKS * SEL, 128), jnp.int32),
             *([tiles] * 14),
             pltpu.VMEM((2, RING, ROW - 1, 2, TILE, HD), jnp.bfloat16),
             pltpu.VMEM((2 * RING * ROW, TILE, HD), jnp.bfloat16),
@@ -379,6 +399,7 @@
             pltpu.VMEM((ROWS, WIDE), jnp.bfloat16),
             dma((ROW - 1,)),
             dma((ROW - 1,)),
+            dma,
             dma,
             dma((2, 2, 4, CHUNKS)),
             dma((2, 2, 4, CHUNKS)),
@@ -402,8 +423,7 @@
         new_values,
         cache_keys.reshape(HELD, TILE, HD),
         cache_values.reshape(HELD, TILE, HD),
-        list_in,
-        slots,
+        tile_lists,
     )
 
 

time: 146 us -> 136 us (0.932)
  Pallas kernels: 141 us -> 134 us
  other arithmetic: 1.49 us -> 0 us
    pallas_call x1, Pallas kernels: 141 us -> 134 us  [on_device(): pl.pallas_call(kernel, out_shape=jax.ShapeDtypeStruct((PART, HEADS * WIDE...]
where the time goes in v2:
time: 136 us; the launch traced here: 135 us
  Pallas kernels  134 us (99%)
  local copies, waits for them, and re-layouts  1.87 us (1%)
    pallas_call x1, Pallas kernels, on_device(): pl.pallas_call(kernel, out_shape=jax.ShapeDtypeStruct((PART, HEADS * WIDE...  134 us

profile of v2, /device:TPU:1, one launch (start us, length us, event | category | flops | bytes accessed | tf_op | source)
XLA Modules:
  0.0 135.4 jit_solution(13520129382047911912)
XLA Ops:
  0.0 133.6 %shard_map.64 = bf16[64,4096]{1,0:T(8,128)(2,1)} custom-call(bf16[64,4096]{1,0:T(8,128)(2,1)} %q_in.1, bf16[64,1024]{1,0:T(8,128)(2,1)} %k_in.1, bf16[64,1024]{1,0:T(8,128)(2,1)} %v_in.1, bf16[16,128,128]{2,1,0:T(8,128)(2,1)} %bitcast.2, bf16[16,128,128]{2,1,0:T(8,128)(2,1)} %bitcast.3, s32[4,1,12]{2,1,0:T(1,128)} %lists.1), custom_call_target="tpu_custom_call" | custom-call | tf_op jit(solution)/shard_map/pallas_call | solution.py:374
  133.6 1.9 %copy.8 = bf16[64,4096]{1,0:T(8,128)(2,1)} copy(bf16[64,4096]{1,0:T(8,128)(2,1)} %shard_map.64) | data formatting | bytes 1048576

commit v3 on v1

v3 whole, which is shorter than its diff:
```python
import functools
import math

import jax
import jax.numpy as jnp
from jax import lax
from jax.experimental import pallas as pl
from jax.experimental.pallas import tpu as pltpu
from jax.sharding import PartitionSpec as P

KV = 8
HD = 128
QB = 128
TILE = 128
SEL = 12
GROUP = 4

RING = 8
ROW = 8
HEADS = 8
HELD = 16
CHUNK = 4
CHUNKS = HELD // CHUNK
BLOCKS = 4
ROWS = BLOCKS * QB
PART = ROWS // HEADS
WIDE = GROUP * HD
HALF = HD // 2
REMOTE = SEL * TILE
KEYS = REMOTE + 2 * QB
NEG_FILL = -1e30
EXP2_SCALE = math.log2(math.e) / math.sqrt(HD)
MESH = pl.DeviceIdType.MESH
ORDER = (2, 1, 3, 0)
SOFT_ROWS = 32


def kernel(
    q_hbm, k_hbm, v_hbm, keys_hbm, values_hbm, lists,
    out,
    q_in, k_in, v_in, key_tiles, value_tiles, q_rows, k_loc, v_loc, list_raw, list_in, row_lists, table, table_smem, slot_table, slots,
    kb1, kb2, kb3, kb4, kb5, kb6, kb7,
    vb1, vb2, vb3, vb4, vb5, vb6, vb7,
    stage, got_k, got_v0, got_v1, gathered, scores, weights, totals, out_stage, out_parts,
    load_sem, list_send, list_recv, plan_sem, slot_sem, y_send, y_recv, x_send, x_recv,
    z_send, z_recv, z_local, prev_send, prev_recv, o_send, o_recv, o_local,
):
    seq = lax.axis_index("seq")
    z = lax.axis_index("head")
    y = seq // ROW
    col = seq % ROW
    ahead = (seq + ROW) % (RING * ROW)
    behind = (seq + (RING - 1) * ROW) % (RING * ROW)
    after = (seq + 1) % (RING * ROW)
    before = (seq + RING * ROW - 1) % (RING * ROW)
    blocks_of = ((key_tiles, kb1, kb2, kb3, kb4, kb5, kb6, kb7), (value_tiles, vb1, vb2, vb3, vb4, vb5, vb6, vb7))
    got_v = (got_v0, got_v1)

    def row_peer(o):
        return y * ROW + (col + o) % ROW

    def head_peer(o):
        return (z + o) % HEADS

    pairs = ((keys_hbm, key_tiles), (q_hbm, q_in), (k_hbm, k_in), (v_hbm, v_in), (values_hbm, value_tiles))
    loads = [pltpu.make_async_copy(src, dst, load_sem.at[i]) for i, (src, dst) in enumerate(pairs)]
    for load in loads:
        load.start()

    barrier = pltpu.get_barrier_semaphore()

    def greet(where):
        pl.semaphore_signal(barrier, inc=1, device_id=where, device_id_type=MESH)

    for o in range(1, ROW):
        greet((row_peer(o), z))
    for o in range(1, HEADS):
        greet((seq, head_peer(o)))
    greet((ahead, z))
    greet((behind, z))
    greet((before, HEADS - 2))
    greet((before, HEADS - 1))
    lane = lax.broadcasted_iota(jnp.int32, (ROW, 128), 1)
    device = lax.broadcasted_iota(jnp.int32, (ROW, 128), 0)
    list_raw[...] = jnp.full((8, 128), -1, jnp.int32)
    for block in range(BLOCKS):
        list_raw[pl.ds(block, 1), pl.ds(0, SEL)] = lists[block]
    raw = list_raw[...]
    flat = jnp.full((8, 128), -1, jnp.int32)
    for block in range(BLOCKS):
        moved = pltpu.roll(jnp.broadcast_to(raw[block : block + 1], (8, 128)), block * SEL, 1)
        flat = jnp.where((lane >= block * SEL) & (lane < (block + 1) * SEL), moved, flat)
    list_in[...] = flat

    is_last = z >= HEADS - 2
    pl.semaphore_wait(barrier, ROW - 1 + HEADS - 1 + 2 + jnp.where(is_last, HEADS, 0))

    def remote(src, dst, send, recv, where):
        return pltpu.make_async_remote_copy(
            src_ref=src, dst_ref=dst, send_sem=send, recv_sem=recv, device_id=where, device_id_type=MESH
        )

    def list_copy(o):
        return remote(list_in, row_lists.at[col], list_send.at[o - 1], list_recv.at[o - 1], (row_peer(o), z))

    def ring_copy(kv, way, hop, chunk):
        refs = blocks_of[kv]
        if way == 0:
            src, dst, where = refs[hop - 1], refs[hop], ahead
        else:
            src, dst, where = refs[(RING - hop + 1) % RING], refs[RING - hop], behind
        part = pl.ds(chunk * CHUNK, CHUNK)
        return remote(
            src.at[part], dst.at[part], y_send.at[kv, way, hop - 1, chunk], y_recv.at[kv, way, hop - 1, chunk], (where, z)
        )

    def row_copy(kind, rel, o):
        if kind == 0:
            src, dst = stage.at[0, rel, o - 1], got_k.at[pl.ds((col * RING + rel) * 2, 2)]
        else:
            src, dst = stage.at[1, rel, o - 1, kind - 1], got_v[kind - 1].at[col * RING + rel]
        return remote(src, dst, x_send.at[kind, rel, o - 1], x_recv.at[kind, rel, o - 1], (row_peer(o), z))

    def head_copies(o):
        to = head_peer(o)
        wide = pl.ds(pl.multiple_of(to * WIDE, WIDE), WIDE)
        narrow = pl.ds(pl.multiple_of(to * HD, HD), HD)
        rows = pl.ds(pl.multiple_of(z * PART, PART), PART)
        new_rows = pl.ds(pl.multiple_of(QB + z * PART, PART), PART)
        triples = ((q_in.at[:, wide], q_rows.at[rows]), (k_in.at[:, narrow], k_loc.at[new_rows]), (v_in.at[:, narrow], v_loc.at[new_rows]))
        if o == 0:
            return [pltpu.make_async_copy(src, dst, z_local.at[i]) for i, (src, dst) in enumerate(triples)]
        return [
            remote(src, dst, z_send.at[i, o - 1], z_recv.at[i, o - 1], (seq, to)) for i, (src, dst) in enumerate(triples)
        ]

    def prior_copies(to):
        source = z % 2
        narrow = pl.ds(to * HD, HD)
        rows = pl.ds(pl.multiple_of(source * PART, PART), PART)
        return [
            remote(k_in.at[:, narrow], k_loc.at[rows], prev_send.at[0, to], prev_recv.at[0, source], (after, to)),
            remote(v_in.at[:, narrow], v_loc.at[rows], prev_send.at[1, to], prev_recv.at[1, source], (after, to)),
        ]

    def forward(kv, hop, chunks):
        for chunk in chunks:
            ring_copy(kv, 0, hop, chunk).start()
            ring_copy(kv, 1, hop, chunk).start()

    for o in range(1, ROW):
        list_copy(o).start()
    loads[0].wait()
    forward(0, 1, range(CHUNKS))

    for o in range(1, ROW):
        list_copy(o).wait()
    row_lists[col] = list_in[...]
    listed = row_lists[0]
    for d in range(1, ROW):
        listed = jnp.where(device == d, row_lists[d], listed)
    plan = jnp.zeros((ROW, 128), jnp.int32)
    for rel in range(RING):
        owner = ((y + RING - rel) % RING) * ROW + col
        mine = lax.shift_right_arithmetic(listed, 4) == owner
        tile = jnp.bitwise_and(listed, HELD - 1)
        smallest = jnp.min(jnp.where(mine, tile, HELD - 1), axis=1, keepdims=True)
        largest = jnp.max(jnp.where(mine, tile, 0), axis=1, keepdims=True)
        plan = jnp.where(lane == 2 * rel, smallest, plan)
        plan = jnp.where(lane == 2 * rel + 1, largest, plan)
    table[...] = plan

    def place_own_list():
        entries = BLOCKS * SEL
        across = jnp.broadcast_to(flat[0:1], (entries, 128))
        lanes = lax.broadcasted_iota(jnp.int32, (entries, 128), 1)
        diagonal = lanes == lax.broadcasted_iota(jnp.int32, (entries, 128), 0)
        down = jnp.max(jnp.where(diagonal, across, 0), axis=1, keepdims=True)
        owner = lax.shift_right_arithmetic(down, 4)
        earlier = (lax.shift_right_arithmetic(across, 4) == owner) & (across < down)
        rank = jnp.max(jnp.where(earlier, 1, 0), axis=1, keepdims=True)
        rel = jnp.bitwise_and(y - lax.shift_right_arithmetic(owner, 3), RING - 1)
        slot = (jnp.bitwise_and(owner, ROW - 1) * RING + rel) * 2 + rank
        slot_table[...] = jnp.broadcast_to(slot, (entries, 128))

    left = lax.broadcasted_iota(jnp.int32, (TILE, HD), 1) < HALF

    def halves(lower, upper):
        turned = pltpu.roll(upper, HALF, 1)
        return jnp.where(left, lower, turned), jnp.where(left, turned, lower)

    def pack(kv, rel):
        source = blocks_of[kv][rel]

        def two(to):
            lower = source[jnp.bitwise_and(table_smem[to, 2 * rel], HELD - 1)]
            upper = source[jnp.bitwise_and(table_smem[to, 2 * rel + 1], HELD - 1)]
            return halves(lower, upper) if kv else (lower, upper)

        def one(o, carry):
            first, second = two((col + o) % ROW)
            stage[kv, rel, o - 1, 0] = first
            stage[kv, rel, o - 1, 1] = second
            return carry

        lax.fori_loop(1, ROW, one, 0)
        first, second = two(col)
        place = col * RING + rel
        if kv:
            got_v0[place] = first
            got_v1[place] = second
        else:
            got_k[2 * place] = first
            got_k[2 * place + 1] = second

    def hand_out(kind, rel):
        for o in range(1, ROW):
            row_copy(kind, rel, o).start()

    def hand_in(kind):
        for rel in range(RING):
            for o in range(1, ROW):
                row_copy(kind, rel, o).wait()

    def pass_on(kv, hop, chunk):
        for way in range(2):
            ring_copy(kv, way, hop, chunk).wait_recv()
            if hop < 3 or (chunk < CHUNKS // 2) == (way == 0):
                ring_copy(kv, way, hop + 1, chunk).start()

    def last_block(kv):
        for chunk in range(CHUNKS // 2):
            ring_copy(kv, 0, 4, chunk).wait_recv()
            ring_copy(kv, 1, 4, CHUNKS // 2 + chunk).wait_recv()
        pack(kv, 4)

    def block_at(step):
        return (z // 2 + step) % BLOCKS

    def gather(block, take):
        def one(j, carry):
            slot = jnp.bitwise_and(slots[block * SEL + j, 0], 2 * RING * ROW - 1)
            gathered[pl.ds(pl.multiple_of(j * TILE, TILE), TILE), :] = take(slot)
            return carry

        lax.fori_loop(0, SEL, one, 0)

    row = lax.broadcasted_iota(jnp.int32, (SOFT_ROWS, 2 * QB), 0)
    column = lax.broadcasted_iota(jnp.int32, (SOFT_ROWS, 2 * QB), 1)

    def score(piece, carry):
        step, head = piece // GROUP, piece % GROUP
        block = block_at(step)
        first_row = pl.multiple_of(block * QB, QB)

        @pl.when(head == 0)
        def _():
            gather(block, lambda slot: got_k[slot])
            gathered[pl.ds(REMOTE, 2 * QB), :] = k_loc[pl.ds(first_row, 2 * QB), :]

        query = q_rows[pl.ds(first_row, QB), pl.ds(pl.multiple_of(head * HD, HD), HD)]
        for pair in range(KEYS // (2 * TILE)):
            part = pl.ds(pair * 2 * TILE, 2 * TILE)
            scores[:, part] = lax.dot_general(
                query, gathered[part, :], (((1,), (1,)), ((), ())), preferred_element_type=jnp.float32
            )
        from_column = jnp.where(block + seq > 0, 0, QB)

        def soften(i, inner):
            first = pl.multiple_of(i * SOFT_ROWS, SOFT_ROWS)
            rows = pl.ds(first, SOFT_ROWS)
            kept = pl.ds(pl.multiple_of(head * QB + first, SOFT_ROWS), SOFT_ROWS)
            visible = (column - QB <= row + first) & (column >= from_column)
            far = scores[rows, pl.ds(0, REMOTE)]
            near = jnp.where(visible, scores[rows, pl.ds(REMOTE, 2 * QB)], NEG_FILL)
            top = jnp.maximum(jnp.max(far, axis=1, keepdims=True), jnp.max(near, axis=1, keepdims=True))
            far = jnp.exp2((far - top) * EXP2_SCALE)
            near = jnp.exp2((near - top) * EXP2_SCALE)
            total = jnp.sum(far, axis=1, keepdims=True) + jnp.sum(near, axis=1, keepdims=True)
            weights[step, kept, pl.ds(0, REMOTE)] = far.astype(jnp.bfloat16)
            weights[step, kept, pl.ds(REMOTE, 2 * QB)] = near.astype(jnp.bfloat16)
            totals[step, kept, :] = jnp.broadcast_to(total, (SOFT_ROWS, HD))
            return inner

        return lax.fori_loop(0, QB // SOFT_ROWS, soften, carry)

    place_own_list()
    copy = pltpu.make_async_copy(table, table_smem, plan_sem)
    copy.start()
    for load in loads[1:]:
        load.wait()
    copy.wait()
    pack(0, 0)
    pack(1, 0)
    hand_out(0, 0)
    pass_on(0, 1, 0)
    hand_out(1, 0)
    hand_out(2, 0)
    pass_on(0, 1, 1)
    for o in range(HEADS):
        for copy in head_copies(o):
            copy.start()

    @pl.when(is_last)
    def _():
        for to in range(HEADS):
            for copy in prior_copies(to):
                copy.start()

    pass_on(0, 1, 2)
    pass_on(0, 1, 3)
    for hop in range(1, 4):
        if hop > 1:
            for chunk in range(CHUNKS):
                pass_on(0, hop, chunk)
                if chunk == 0:
                    hand_out(0, RING - hop + 1)
        pack(0, hop)
        pack(0, RING - hop)
        hand_out(0, hop)
    forward(1, 1, range(CHUNKS))
    copy = pltpu.make_async_copy(slot_table, slots, slot_sem)
    copy.start()
    copy.wait()
    hand_out(0, 5)
    last_block(0)

    pass_on(1, 1, 0)
    hand_out(0, 4)
    for chunk in range(1, CHUNKS):
        pass_on(1, 1, chunk)
    for o in range(HEADS):
        for copy in head_copies(o):
            copy.wait()
    for source in range(2):
        rows = pl.ds(source * PART, PART)
        for kv, ref in enumerate((k_loc, v_loc)):
            pltpu.make_async_copy(ref.at[rows], ref.at[rows], prev_recv.at[kv, source]).wait()
    pack(1, 1)
    pack(1, 7)
    hand_out(1, 1)
    hand_out(2, 1)
    done = 0
    for hop in range(2, 4):
        for chunk in range(CHUNKS):
            pass_on(1, hop, chunk)
            if hop == 2 and chunk == 0:
                hand_out(1, 7)
                hand_out(2, 7)
                continue
            if hop == 2 and chunk == 1:
                hand_in(0)
            if hop == 3 and chunk == 0:
                hand_out(1, 6)
                hand_out(2, 6)
            lax.fori_loop(done, done + 2, score, 0)
            done += 2
        pack(1, hop)
        pack(1, RING - hop)
        hand_out(1, hop)
        if hop == 2:
            hand_out(2, hop)
    hand_out(1, 5)
    lax.fori_loop(done, BLOCKS * GROUP, score, 0)
    last_block(1)
    hand_out(2, 3)
    hand_out(1, 4)
    hand_out(2, 5)
    hand_out(2, 4)

    def attend(step, half):
        block = block_at(step)
        first_row = pl.multiple_of(block * QB, QB)

        def take(slot):
            on_left = jnp.bitwise_and(slot, 1) == half
            return jnp.where(left == on_left, got_v[half][lax.shift_right_logical(slot, 1)], zero)

        zero = jnp.zeros((TILE, HD), jnp.bfloat16)
        gather(block, take)
        near = v_loc[pl.ds(first_row, 2 * QB), :]
        near_left = lax.broadcasted_iota(jnp.int32, (2 * QB, HD), 1) < HALF
        gathered[pl.ds(REMOTE, 2 * QB), :] = jnp.where(near_left == (half == 0), near, jnp.zeros_like(near))
        sides = jnp.dot(weights[step], gathered[...], preferred_element_type=jnp.float32)
        result = ((sides + pltpu.roll(sides, HALF, 1)) / totals[step]).astype(jnp.bfloat16)
        for pair in range(GROUP // 2):
            even, odd = result[2 * pair * QB : (2 * pair + 1) * QB], result[(2 * pair + 1) * QB : (2 * pair + 2) * QB]
            out_stage[half, pl.ds(first_row, QB), pl.ds(pair * HD, HD)] = jnp.where(left, even, odd)

    def return_copy(step, half, to, place):
        rows = pl.ds(pl.multiple_of(to * PART, PART), PART)
        part = pl.ds(pl.multiple_of(z * (WIDE // 2), WIDE // 2), WIDE // 2)
        src, dst = out_stage.at[half, rows], out_parts.at[half, :, part]
        if place is None:
            return pltpu.make_async_copy(src, dst, o_local.at[half])
        return remote(src, dst, o_send.at[half, place], o_recv.at[half, place], (seq, to))

    returns = []
    for half in range(2):
        hand_in(1 + half)
        for step in ORDER:
            attend(step, half)
            if step != 0:
                for parity in range(2):
                    to = 2 * block_at(step) + parity
                    returns.append(return_copy(step, half, to, 2 * step + (z + parity) % 2))
            else:
                returns.append(return_copy(step, half, z + 1 - 2 * (z % 2), 0))
                returns.append(return_copy(step, half, z, None))
            returns[-2].start()
            returns[-1].start()
    for copy in returns:
        copy.wait()

    part_left = lax.broadcasted_iota(jnp.int32, (PART, HD), 1) < HALF
    for pair in range(HEADS * GROUP // 2):
        lanes = pl.ds(pair * HD, HD)
        first, second = out_parts[0, :, lanes], out_parts[1, :, lanes]
        out[:, pl.ds(2 * pair * HD, HD)] = jnp.where(part_left, first, pltpu.roll(second, HALF, 1))
        out[:, pl.ds((2 * pair + 1) * HD, HD)] = jnp.where(part_left, pltpu.roll(first, HALF, 1), second)

    for kv in range(2):
        for hop in range(1, 5):
            for chunk in range(CHUNKS):
                for way in range(2):
                    if hop < 4 or (chunk < CHUNKS // 2) == (way == 0):
                        ring_copy(kv, way, hop, chunk).wait_send()

    @pl.when(is_last)
    def _():
        for to in range(HEADS):
            for copy in prior_copies(to):
                copy.wait_send()


def on_device(queries, new_keys, new_values, cache_keys, cache_values, tile_lists):
    tiles = pltpu.VMEM((HELD, TILE, HD), jnp.bfloat16)
    dma = pltpu.SemaphoreType.DMA
    vmem = pl.BlockSpec(memory_space=pltpu.VMEM)
    return pl.pallas_call(
        kernel,
        out_shape=pltpu.VMEM((PART, HEADS * WIDE), jnp.bfloat16),
        in_specs=[pl.BlockSpec(memory_space=pl.ANY)] * 5 + [vmem],
        out_specs=vmem,
        scratch_shapes=[
            pltpu.VMEM((PART, HEADS * WIDE), jnp.bfloat16),
            pltpu.VMEM((PART, HEADS * HD), jnp.bfloat16),
            pltpu.VMEM((PART, HEADS * HD), jnp.bfloat16),
            tiles,
            tiles,
            pltpu.VMEM((ROWS, WIDE), jnp.bfloat16),
            pltpu.VMEM((QB + ROWS, HD), jnp.bfloat16),
            pltpu.VMEM((QB + ROWS, HD), jnp.bfloat16),
            pltpu.VMEM((8, 128), jnp.int32),
            pltpu.VMEM((8, 128), jnp.int32),
            pltpu.VMEM((ROW, 8, 128), jnp.int32),
            pltpu.VMEM((ROW, 128), jnp.int32),
            pltpu.SMEM((ROW, 128), jnp.int32),
            pltpu.VMEM((BLOCKS * SEL, 128), jnp.int32),
            pltpu.SMEM((BLOCKS * SEL, 128), jnp.int32),
            *([tiles] * 14),
            pltpu.VMEM((2, RING, ROW - 1, 2, TILE, HD), jnp.bfloat16),
            pltpu.VMEM((2 * RING * ROW, TILE, HD), jnp.bfloat16),
            pltpu.VMEM((RING * ROW, TILE, HD), jnp.bfloat16),
            pltpu.VMEM((RING * ROW, TILE, HD), jnp.bfloat16),
            pltpu.VMEM((KEYS, HD), jnp.bfloat16),
            pltpu.VMEM((QB, KEYS), jnp.float32),
            pltpu.VMEM((BLOCKS, GROUP * QB, KEYS), jnp.bfloat16),
            pltpu.VMEM((BLOCKS, GROUP * QB, HD), jnp.float32),
            pltpu.VMEM((2, ROWS, WIDE // 2), jnp.bfloat16),
            pltpu.VMEM((2, PART, HEADS * WIDE // 2), jnp.bfloat16),
            dma((5,)),
            dma((ROW - 1,)),
            dma((ROW - 1,)),
            dma,
            dma,
            dma((2, 2, 4, CHUNKS)),
            dma((2, 2, 4, CHUNKS)),
            dma((3, RING, ROW - 1)),
            dma((3, RING, ROW - 1)),
            dma((3, HEADS - 1)),
            dma((3, HEADS - 1)),
            dma((3,)),
            dma((2, HEADS)),
            dma((2, 2)),
            dma((2, HEADS)),
            dma((2, HEADS)),
            dma((2,)),
        ],
        compiler_params=pltpu.CompilerParams(
            collective_id=0, has_side_effects=True, vmem_limit_bytes=64000 * 1024
        ),
    )(
        queries,
        new_keys,
        new_values,
        cache_keys.reshape(HELD, TILE, HD),
        cache_values.reshape(HELD, TILE, HD),
        tile_lists,
    )


def solution(mesh):
    return jax.shard_map(
        on_device,
        mesh=mesh,
        in_specs=(
            P(("seq", "head"), None),
            P(("seq", "head"), None),
            P(("seq", "head"), None),
            P("seq", "head"),
            P("seq", "head"),
            P("seq", "head", None),
        ),
        out_specs=P(("seq", "head"), None),
        check_vma=False,
    )
```

time: 146 us -> 132 us (0.904)
  Pallas kernels: 141 us -> 131 us
  local copies, waits for them, and re-layouts: 3.24 us -> 0.8 us
  other arithmetic: 1.49 us -> 0 us
    pallas_call x1, Pallas kernels: 141 us -> 131 us  [on_device(): pl.pallas_call(kernel, out_shape=pltpu.VMEM((PART, HEADS * WIDE), jnp.bfl...]
    unnamed x4 -> x1, local copies, waits for them, and re-layouts: 2.55 us -> 0.8 us
where the time goes in v3:
time: 132 us
  Pallas kernels  131 us (99%)
    pallas_call x1, Pallas kernels, on_device(): pl.pallas_call(kernel, out_shape=pltpu.VMEM((PART, HEADS * WIDE), jnp.bfl...  131 us

profile of v3, /device:TPU:1, one launch (start us, length us, event | category | flops | bytes accessed | tf_op | source)
XLA Modules:
  0.0 131.6 jit_solution(13111402638790337004)
XLA Ops:
  0.0 130.8 %shard_map.64 = bf16[64,4096]{1,0:T(8,128)(2,1)S(1)} custom-call(bf16[64,4096]{1,0:T(8,128)(2,1)} %q_hbm.1, bf16[64,1024]{1,0:T(8,128)(2,1)} %k_hbm.1, bf16[64,1024]{1,0:T(8,128)(2,1)} %v_hbm.1, bf16[16,128,128]{2,1,0:T(8,128)(2,1)} %bitcast.2, bf16[16,128,128]{2,1,0:T(8,128)(2,1)} %bitcast.3, s32[4,1,12]{2,1,0:T(1,128)} %lists.1), custom_call_target="tpu_custom_call" | custom-call | tf_op jit(solution)/shard_map/pallas_call | solution.py:440
  130.8 0.8 copy.8

commit v4 on v3

--- a/solution.py
+++ b/solution.py
@@ -203,7 +203,7 @@
             stage[kv, rel, o - 1, 1] = second
             return carry
 
-        lax.fori_loop(1, ROW, one, 0)
+        lax.fori_loop(1, ROW, one, 0, unroll=True)
         first, second = two(col)
         place = col * RING + rel
         if kv:
@@ -243,7 +243,7 @@
             gathered[pl.ds(pl.multiple_of(j * TILE, TILE), TILE), :] = take(slot)
             return carry
 
-        lax.fori_loop(0, SEL, one, 0)
+        lax.fori_loop(0, SEL, one, 0, unroll=True)
 
     row = lax.broadcasted_iota(jnp.int32, (SOFT_ROWS, 2 * QB), 0)
     column = lax.broadcasted_iota(jnp.int32, (SOFT_ROWS, 2 * QB), 1)

time: 132 us -> 130 us (0.985)
  Pallas kernels: 131 us -> 129 us
    pallas_call x1, Pallas kernels: 131 us -> 129 us  [on_device(): pl.pallas_call(kernel, out_shape=pltpu.VMEM((PART, HEADS * WIDE), jnp.bfl...]
where the time goes in v4:
time: 130 us
  Pallas kernels  129 us (99%)
    pallas_call x1, Pallas kernels, on_device(): pl.pallas_call(kernel, out_shape=pltpu.VMEM((PART, HEADS * WIDE), jnp.bfl...  129 us

profile of v4, /device:TPU:1, one launch (start us, length us, event | category | flops | bytes accessed | tf_op | source)
XLA Modules:
  0.0 129.8 jit_solution(5610483833333366914)
XLA Ops:
  0.0 129.0 %shard_map.64 = bf16[64,4096]{1,0:T(8,128)(2,1)S(1)} custom-call(bf16[64,4096]{1,0:T(8,128)(2,1)} %q_hbm.1, bf16[64,1024]{1,0:T(8,128)(2,1)} %k_hbm.1, bf16[64,1024]{1,0:T(8,128)(2,1)} %v_hbm.1, bf16[16,128,128]{2,1,0:T(8,128)(2,1)} %bitcast.2, bf16[16,128,128]{2,1,0:T(8,128)(2,1)} %bitcast.3, s32[4,1,12]{2,1,0:T(1,128)} %lists.1), custom_call_target="tpu_custom_call" | custom-call | tf_op jit(solution)/shard_map/pallas_call | solution.py:440
  129.0 0.8 copy.8

commit v5 on v4

--- a/solution.py
+++ b/solution.py
@@ -31,7 +31,7 @@
 NEG_FILL = -1e30
 EXP2_SCALE = math.log2(math.e) / math.sqrt(HD)
 MESH = pl.DeviceIdType.MESH
-ORDER = (2, 1, 3, 0)
+ORDER = (1, 3, 2, 0)
 SOFT_ROWS = 32
 
 
@@ -41,7 +41,7 @@
     q_in, k_in, v_in, key_tiles, value_tiles, q_rows, k_loc, v_loc, list_raw, list_in, row_lists, table, table_smem, slot_table, slots,
     kb1, kb2, kb3, kb4, kb5, kb6, kb7,
     vb1, vb2, vb3, vb4, vb5, vb6, vb7,
-    stage, got_k, got_v0, got_v1, gathered, scores, weights, totals, out_stage, out_parts,
+    stage, got_k, got_v0, got_v1, gathered, scores, weights, inverses, out_stage, out_parts,
     load_sem, list_send, list_recv, plan_sem, slot_sem, y_send, y_recv, x_send, x_recv,
     z_send, z_recv, z_local, prev_send, prev_recv, o_send, o_recv, o_local,
 ):
@@ -279,7 +279,7 @@
             total = jnp.sum(far, axis=1, keepdims=True) + jnp.sum(near, axis=1, keepdims=True)
             weights[step, kept, pl.ds(0, REMOTE)] = far.astype(jnp.bfloat16)
             weights[step, kept, pl.ds(REMOTE, 2 * QB)] = near.astype(jnp.bfloat16)
-            totals[step, kept, :] = jnp.broadcast_to(total, (SOFT_ROWS, HD))
+            inverses[step, kept, :] = jnp.broadcast_to(1.0 / total, (SOFT_ROWS, HD))
             return inner
 
         return lax.fori_loop(0, QB // SOFT_ROWS, soften, carry)
@@ -382,7 +382,7 @@
         near_left = lax.broadcasted_iota(jnp.int32, (2 * QB, HD), 1) < HALF
         gathered[pl.ds(REMOTE, 2 * QB), :] = jnp.where(near_left == (half == 0), near, jnp.zeros_like(near))
         sides = jnp.dot(weights[step], gathered[...], preferred_element_type=jnp.float32)
-        result = ((sides + pltpu.roll(sides, HALF, 1)) / totals[step]).astype(jnp.bfloat16)
+        result = ((sides + pltpu.roll(sides, HALF, 1)) * inverses[step]).astype(jnp.bfloat16)
         for pair in range(GROUP // 2):
             even, odd = result[2 * pair * QB : (2 * pair + 1) * QB], result[(2 * pair + 1) * QB : (2 * pair + 2) * QB]
             out_stage[half, pl.ds(first_row, QB), pl.ds(pair * HD, HD)] = jnp.where(left, even, odd)

time: 130 us -> 130 us (level)
  no operation moved by 1% of the time
where the time goes in v5:
time: 130 us; the launch traced here: 129 us
  Pallas kernels  129 us (99%)
    pallas_call x1, Pallas kernels, on_device(): pl.pallas_call(kernel, out_shape=pltpu.VMEM((PART, HEADS * WIDE), jnp.bfl...  129 us

profile of v5, /device:TPU:1, one launch (start us, length us, event | category | flops | bytes accessed | tf_op | source)
XLA Modules:
  0.0 129.5 jit_solution(12239166302439308986)
XLA Ops:
  0.0 128.7 %shard_map.64 = bf16[64,4096]{1,0:T(8,128)(2,1)S(1)} custom-call(bf16[64,4096]{1,0:T(8,128)(2,1)} %q_hbm.1, bf16[64,1024]{1,0:T(8,128)(2,1)} %k_hbm.1, bf16[64,1024]{1,0:T(8,128)(2,1)} %v_hbm.1, bf16[16,128,128]{2,1,0:T(8,128)(2,1)} %bitcast.2, bf16[16,128,128]{2,1,0:T(8,128)(2,1)} %bitcast.3, s32[4,1,12]{2,1,0:T(1,128)} %lists.1), custom_call_target="tpu_custom_call" | custom-call | tf_op jit(solution)/shard_map/pallas_call | solution.py:440
  128.7 0.8 copy.8
